TPU v7x, 32 devices: a whole 2x2x4 slice. The times are simulated.
32 devices in a mesh: wall: 4 (over y, core), surf: 8 (over z, x).
Axes of the slice: x: 2, y: 2, z: 4, core: 2. Of those that a mesh axis runs over, the one named last changes fastest.
Arguments:
- vector: bfloat16 [32, 16, 320, 256], P('surf', 'wall'), may hold values from -40 to 40
- lengths: int32 [32], P('surf'), may hold values from 1 to 16, as said below
- north_of: int32 [8, 4], P('surf'), may hold values from 0 to 3, each once within a row
- diagonal: bfloat16 [32, 16, 320, 320], P('surf', 'wall'), may hold values from -1 to 8
- lifting: bfloat16 [32, 16, 6, 80, 320], P('surf', 'wall'), may hold values from -0.625 to 0.625
- inverse_rows: bfloat16 [32, 16, 80, 320], P('surf', 'wall'), may hold values from -0.25 to 0.25
Outputs:
- next_basis: bfloat16 [32, 16, 320, 256], P('surf', 'wall')
- coefs: float32 [2, 256], replicated
Inputs may be any that keep to these rules, and one draw needn't show every extreme that they name: `lengths`: in every patch of 4 lines one line has 16 elements and another has 1.
All inputs are finite; a program needn't handle non-finite values.
Results may differ from a plain program's by a relative error of at most 0.00135.
Values may be sent and summed in bfloat16 or wider, within the bound.
A program may use at most 64 MiB of HBM per device.

v0:
```python
import jax
import jax.numpy as jnp
from jax import lax
from jax.sharding import PartitionSpec as P

VARS = 5
NODE1D = 4
FACE = 80


FULL_ACCURACY = lax.Precision.HIGHEST


def with_halo(cells, sides, width, closed):
    for axis, dim in sides:
        count = lax.axis_size(axis)
        ends = count if closed else count - 1
        head = lax.slice_in_dim(cells, 0, width, axis=dim)
        tail = lax.slice_in_dim(cells, cells.shape[dim] - width, cells.shape[dim], axis=dim)
        cells = jnp.concatenate(
            [
                lax.ppermute(tail, axis, [(i, (i + 1) % count) for i in range(ends)]),
                cells,
                lax.ppermute(head, axis, [((i + 1) % count, i) for i in range(ends)]),
            ],
            axis=dim,
        )
    return cells


def from_behind(shard, axis, by):
    devices = lax.axis_size(axis)
    pairs = [(i, i + by) for i in range(devices) if 0 <= i + by < devices]
    return lax.ppermute(shard, axis, pairs)


def face_traces(values):
    leading = values.shape[:-2]
    column_entries = values.shape[-1]
    nodal_cube = values.reshape(leading + (VARS, NODE1D, NODE1D, NODE1D, column_entries))
    last_node = NODE1D - 1

    def flatten(piece):
        return piece.reshape(leading + (FACE, column_entries))

    bottom_face = flatten(nodal_cube[..., 0, :])
    top_face = flatten(nodal_cube[..., last_node, :])
    west_face = flatten(nodal_cube[..., 0, :, :, :])
    east_face = flatten(nodal_cube[..., last_node, :, :, :])
    south_face = flatten(nodal_cube[..., 0, :, :])
    north_face = flatten(nodal_cube[..., last_node, :, :])
    return (bottom_face, top_face, west_face, east_face, south_face, north_face)


def exact_times(form, left, right):
    return jnp.einsum(
        form, left.astype(jnp.float32), right.astype(jnp.float32), precision=FULL_ACCURACY
    )


def apply_map(matrices, states):
    return exact_times("lfg,lgr->lfr", matrices, states)


def per_device(vector, lengths, north_of, diagonal, lifting, inverse_rows):
    lines_here, segment, block_size, column_entries = vector.shape
    face_size = inverse_rows.shape[2]
    positions = lax.axis_index("wall") * segment + jnp.arange(segment, dtype=jnp.int32)
    alive_mask = positions[None, :] < lengths[:, None]
    living = alive_mask.astype(jnp.float32)
    masked = vector * alive_mask.astype(jnp.bfloat16)[:, :, None, None]
    bottom_face, top_face, west_face, east_face, south_face, north_face = face_traces(masked)
    wall_edges = jnp.stack([bottom_face[:, 0], top_face[:, -1]], axis=1)
    wall_padded = with_halo(wall_edges, (("wall", 1),), 1, False)
    from_below = jnp.concatenate([wall_padded[:, 0:1], top_face[:, :-1]], axis=1)
    from_above = jnp.concatenate([bottom_face[:, 1:], wall_padded[:, 3:4]], axis=1)
    patch_edges = jnp.stack([west_face[0], east_face[-1]], axis=0)
    patch_padded = with_halo(patch_edges, (("surf", 0),), 1, True)
    from_west = jnp.concatenate([patch_padded[0:1], east_face[:-1]], axis=0)
    from_east = jnp.concatenate([west_face[1:], patch_padded[3:4]], axis=0)
    selector = (north_of[0][:, None] == jnp.arange(lines_here, dtype=jnp.int32)[None, :]).astype(
        jnp.bfloat16
    )
    from_north = jnp.einsum(
        "ij,jsfr->isfr", selector, south_face, preferred_element_type=jnp.float32
    ).astype(jnp.bfloat16)
    from_south = jnp.einsum(
        "ij,isfr->jsfr", selector, north_face, preferred_element_type=jnp.float32
    ).astype(jnp.bfloat16)
    neighbours = jnp.stack(
        [from_below, from_above, from_west, from_east, from_south, from_north], axis=2
    )
    matrix_product = jnp.einsum(
        "lsbc,lscr->lsbr", diagonal, masked, preferred_element_type=jnp.float32
    )
    matrix_product = matrix_product + jnp.einsum(
        "lsgfb,lsgfr->lsbr", lifting, neighbours, preferred_element_type=jnp.float32
    )
    matrix_product = matrix_product * living[:, :, None, None]
    lower_lift = lifting[:, :, 0]
    identity_map = jnp.broadcast_to(
        jnp.eye(face_size, dtype=jnp.float32), (lines_here, face_size, face_size)
    )
    carried = jnp.zeros((lines_here, face_size, column_entries), jnp.float32)
    prefix = identity_map
    free_part = []
    prefixes = []
    for position in range(segment):
        alive_now = living[:, position][:, None, None]
        eliminated = alive_now * (
            matrix_product[:, position]
            - exact_times("lfb,lfr->lbr", lower_lift[:, position], carried)
        )
        free_part.append(eliminated)
        prefixes.append(prefix)
        carried = exact_times("lfb,lbr->lfr", inverse_rows[:, position], eliminated)
        step_map = -alive_now * exact_times(
            "lfb,lgb->lfg", inverse_rows[:, position], lower_lift[:, position]
        )
        prefix = exact_times("lfg,lgh->lfh", step_map, prefix)
    whole_map = prefix
    offset = carried
    wall_count = lax.axis_size("wall")

    def advance(turn_index, received):
        outgoing = apply_map(whole_map, received) + offset
        return from_behind(outgoing, "wall", 1)

    incoming = lax.fori_loop(0, wall_count - 1, advance, jnp.zeros_like(offset))
    finished = []
    for position in range(segment):
        alive_now = living[:, position][:, None, None]
        arriving = apply_map(prefixes[position], incoming)
        correction = exact_times("lfb,lfr->lbr", lower_lift[:, position], arriving)
        finished.append(free_part[position] - alive_now * correction)
    eliminated = jnp.stack(finished, axis=1)
    masked_wide = masked.astype(jnp.float32)
    entries = lines_here * segment * block_size * lax.axis_size("surf") * lax.axis_size("wall")
    coupling_total, self_sum = lax.psum(
        (
            jnp.sum(masked_wide * eliminated, axis=(0, 1, 2)),
            jnp.sum(masked_wide * masked_wide, axis=(0, 1, 2)),
        ),
        ("wall", "surf"),
    )
    projection = coupling_total / self_sum
    remainder = eliminated - projection * masked_wide
    squares = lax.psum(jnp.sum(remainder * remainder, axis=(0, 1, 2)), ("wall", "surf"))
    spread = jnp.sqrt(squares / entries + 1e-06)
    next_basis = (remainder / spread).astype(jnp.bfloat16)
    return (next_basis, jnp.stack([projection, spread]))


def solution(mesh):
    in_specs = (
        P("surf", "wall", None, None),
        P("surf"),
        P("surf", None),
        P("surf", "wall", None, None),
        P("surf", "wall", None, None, None),
        P("surf", "wall", None, None),
    )
    out_specs = (P("surf", "wall", None, None), P())
    return jax.shard_map(
        per_device, mesh=mesh, in_specs=in_specs, out_specs=out_specs, check_vma=False
    )
```

profile of v0, /device:TPU:0, one launch (start us, length us, event | category | flops | bytes accessed | tf_op | source)
XLA Modules:
  0.0 194.8 jit_solution(14934975038232348811)
XLA Ops:
  1.4 3.5 %copy_multiply_fusion = bf16[4,4,320,256]{3,2,0,1:T(8,128)(2,1)} fusion(bf16[4,4,320,256]{3,2,1,0:T(8,128)(2,1)} %param.8, bf16[4,4]{0,1:T(4,128)(2,1)S(1)} %get-tuple-element.58), kind=kLoop, calls=%fused_computation.17 | loop fusion | flops 1310720 | bytes 5242912 | tf_op jit(solution)/shard_map/mul | solution.py:71
  4.8 3.5 %reshape.104 = bf16[4,4,5,4,4,4,256]{6,5,4,3,2,0,1:T(4,128)(2,1)S(1)} reshape(bf16[4,4,320,256]{3,2,0,1:T(8,128)(2,1)} %copy_multiply_fusion) | data formatting | bytes 5242880 | tf_op jit(solution)/shard_map/reshape | solution.py:40
  8.4 3.0 %fusion.77 = (bf16[4,4,5,4,4,1,256]{6,5,4,3,2,0,1:T(2,128)(2,1)S(1)}, bf16[4,4,5,4,4,1,256]{6,5,4,3,2,0,1:T(2,128)(2,1)S(1)}) fusion(bf16[4,4,5,4,4,4,256]{6,5,4,3,2,0,1:T(4,128)(2,1)S(1)} %reshape.104), kind=kLoop, calls=%fused_computation.121 | loop fusion | bytes 2621440 | tf_op jit(solution)/shard_map/slice | solution.py:46
  11.4 1.0 copy.27
  13.1 3.1 %collective-permute-start.1 = (bf16[4,1,80,256]{3,0,2,1:T(4,128)(2,1)}, bf16[4,1,80,256]{3,0,2,1:T(4,128)(2,1)}, u32[]{:S(2)}, u32[]{:S(2)}) collective-permute-start(bf16[4,1,80,256]{3,0,2,1:T(4,128)(2,1)} %slice.155), channel_id=1, source_target_pairs={{0,8},{8,16},{16,24},{1,9},{9,17},{17,25},{2,10},{10,18},{18,26},{... | collective-permute-start | bytes 491528 | tf_op jit(solution)/shard_map/ppermute | solution.py:22
  16.1 1.0 copy.28
  17.9 1.3 collective-permute-start.2
  19.4 1.0 copy.30
  20.4 2.3 %collective-permute-start.3 = (bf16[1,4,80,256]{3,0,2,1:T(2,128)(2,1)}, bf16[1,4,80,256]{3,0,2,1:T(2,128)(2,1)}, u32[]{:S(2)}, u32[]{:S(2)}) collective-permute-start(bf16[1,4,80,256]{3,0,2,1:T(2,128)(2,1)} %copy.30), channel_id=1, source_target_pairs={{0,1},{1,2},{2,3},{3,4},{4,5},{5,6},{6,7},{7,0},{8,9},{9,10},{10,1... | collective-permute-start | bytes 491528 | tf_op jit(solution)/shard_map/ppermute | solution.py:22
  22.8 1.0 copy.34
  23.8 3.0 %collective-permute-start.4 = (bf16[1,4,80,256]{3,0,2,1:T(2,128)(2,1)}, bf16[1,4,80,256]{3,0,2,1:T(2,128)(2,1)}, u32[]{:S(2)}, u32[]{:S(2)}) collective-permute-start(bf16[1,4,80,256]{3,0,2,1:T(2,128)(2,1)} %copy.34), channel_id=1, source_target_pairs={{1,0},{2,1},{3,2},{4,3},{5,4},{6,5},{7,6},{0,7},{9,8},{10,9},{11,1... | collective-permute-start | bytes 491528 | tf_op jit(solution)/shard_map/ppermute | solution.py:24
  26.8 1.4 fusion.75
  28.2 1.4 fusion.74
  29.6 1.3 copy_bitcast_fusion
  33.1 0.9 slice.156
  34.1 1.0 slice.158
  35.1 1.2 copy.31
  36.3 1.4 copy.32
  37.7 1.2 copy.35
  38.9 1.2 copy.37
  40.1 1.3 fusion.35
  41.5 1.5 fusion.36
  43.0 1.7 fusion.37
  44.8 1.7 fusion.38
  46.5 0.8 fusion.32
  48.1 4.8 %fusion.5 = f32[4,4,256,320,1]{2,3,4,1,0:T(8,128)S(1)} fusion(bf16[4,4,6,80,320]{4,3,2,1,0:T(8,128)(2,1)} %param.12, bf16[4,4,6,80,256]{4,0,3,1,2:T(4,128)(2,1)S(1)} %fusion.34), kind=kOutput, calls=%fused_computation.13 | convolution fusion | flops 1258291200 | bytes 14090240 | tf_op jit(solution)/shard_map/lsgfb,lsgfr->lsbr/dot_general | solution.py:96
  52.9 3.7 %fusion.4 = f32[4,4,320,256]{3,2,1,0:T(8,128)S(1)} fusion(f32[4,4,256,320,1]{2,3,4,1,0:T(8,128)S(1)} %fusion.5, f32[4,4]{1,0:T(4,128)S(1)} %copy.39, bf16[4,4,320,320]{3,2,1,0:T(8,128)(2,1)} %param.11, bf16[4,4,320,256]{3,2,0,1:T(8,128)(2,1)S(1)} %copy-done.1), kind=kOutput, calls=%fused_computation.10 | convolution fusion | flops 841482240 | bytes 16384064 | tf_op jit(solution)/shard_map/lsbc,lscr->lsbr/dot_general | solution.py:93
  58.7 1.8 fusion.28
  63.9 1.0 copy-done.6
  65.7 25.3 %while.10 = (s32[]{:T(128)}, f32[4,80,256]{2,1,0:T(8,128)S(1)}, f32[4,80,80]{2,1,0:T(8,128)S(1)}, f32[4,80,256]{2,1,0:T(8,128)S(1)}, s32[]{:T(128)}) while((s32[]{:T(128)}, f32[4,80,256]{2,1,0:T(8,128)S(1)}, f32[4,80,80]{2,1,0:T(8,128)S(1)}, f32[4,80,256]{2,1,0:T(8,128)S(1)}, s32[]{:T(128)}) %tuple.36), condition=%wide.region_1.0_spmd, body=%wide.region_0.0_spmd.sunk | while | flops 78725120 | bytes 2396261 | solution.py:129
  65.7 1.1 convolution_add_fusion.2
  66.8 3.4 %collective-permute-start = (f32[4,80,256]{2,1,0:T(8,128)}, f32[4,80,256]{2,1,0:T(8,128)S(1)}, u32[]{:S(2)}, u32[]{:S(2)}) collective-permute-start(f32[4,80,256]{2,1,0:T(8,128)} %convolution_add_fusion.2), channel_id=1, source_target_pairs={{0,8},{8,16},{16,24},{1,9},{9,17},{17,25},{2,10},{10,18},{18,26},{... | collective-permute-start | bytes 983048 | tf_op jit(solution)/shard_map/while/body/eval_jaxpr/ppermute | solution.py:34
  70.3 1.4 collective-permute-done
  71.7 1.1 convolution_add_fusion.2
  72.8 7.0 %collective-permute-start = (f32[4,80,256]{2,1,0:T(8,128)}, f32[4,80,256]{2,1,0:T(8,128)S(1)}, u32[]{:S(2)}, u32[]{:S(2)}) collective-permute-start(f32[4,80,256]{2,1,0:T(8,128)} %convolution_add_fusion.2), channel_id=1, source_target_pairs={{0,8},{8,16},{16,24},{1,9},{9,17},{17,25},{2,10},{10,18},{18,26},{... | collective-permute-start | bytes 983048 | tf_op jit(solution)/shard_map/while/body/eval_jaxpr/ppermute | solution.py:34
  79.8 1.4 collective-permute-done
  81.2 1.1 convolution_add_fusion.2
  82.4 7.2 %collective-permute-start = (f32[4,80,256]{2,1,0:T(8,128)}, f32[4,80,256]{2,1,0:T(8,128)S(1)}, u32[]{:S(2)}, u32[]{:S(2)}) collective-permute-start(f32[4,80,256]{2,1,0:T(8,128)} %convolution_add_fusion.2), channel_id=1, source_target_pairs={{0,8},{8,16},{16,24},{1,9},{9,17},{17,25},{2,10},{10,18},{18,26},{... | collective-permute-start | bytes 983048 | tf_op jit(solution)/shard_map/while/body/eval_jaxpr/ppermute | solution.py:34
  89.6 1.4 collective-permute-done
  91.4 1.3 fusion.81
  92.7 1.3 fusion.82
  94.1 1.3 fusion.83
  99.6 1.6 fusion.1
  101.2 43.8 %all-reduce = (f32[256]{0:T(256)S(1)}, f32[256]{0:T(256)S(1)}) all-reduce(f32[256]{0:T(256)S(1)} %get-tuple-element.30, f32[256]{0:T(256)S(1)} %get-tuple-element.29), channel_id=1, replica_groups=mesh['wall'=4,'surf'=8] {'wall','surf'}, use_global_device_ids=true, to_apply=%region_3.0 | all-reduce | flops 512 | bytes 4096 | tf_op jit(solution)/shard_map/psum | solution.py:139
  145.0 3.1 %multiply_reduce_fusion = f32[256]{0:T(256)S(1)} fusion(f32[256]{0:T(256)S(1)} %div.17, f32[4,1,320,256]{3,2,0,1:T(8,128)} %copy-done.5, f32[4,1,320,256]{3,2,0,1:T(8,128)} %copy-done.4, f32[4,1,320,256]{3,2,0,1:T(8,128)} %copy-done.3, f32[4,1,320,256]{3,2,0,1:T(8,128)} %copy-done.2, bf16[4,4]{0,1:T(4,128)(2,1)S(1)} %get-tuple-element.58, ...), kind=kLoop, calls=%fused_computation.12 | loop fusion | flops 11796224 | bytes 7866400 | tf_op jit(solution)/shard_map/reduce_sum | solution.py:148
  148.1 41.3 %psum.23 = f32[256]{0:T(256)S(1)} all-reduce(f32[256]{0:T(256)S(1)} %multiply_reduce_fusion), channel_id=1, replica_groups=mesh['wall'=4,'surf'=8] {'wall','surf'}, use_global_device_ids=true, to_apply=%region_7.0 | all-reduce | flops 256 | bytes 2048 | tf_op jit(solution)/shard_map/psum | solution.py:148
  189.5 3.0 %divide_convert_fusion = bf16[4,4,320,256]{3,2,0,1:T(8,128)(2,1)S(1)} fusion(f32[256]{0:T(256)S(1)} %add_sqrt_fusion, f32[256]{0:T(256)S(1)} %div.17, f32[4,1,320,256]{3,2,0,1:T(8,128)} %copy-done.5, f32[4,1,320,256]{3,2,0,1:T(8,128)} %copy-done.4, f32[4,1,320,256]{3,2,0,1:T(8,128)} %copy-done.3, f32[4,1,320,256]{3,2,0,1:T(8,128)} %copy-done.2, ...), kind=kLoop, calls=%fused_computation.11 | loop fusion | flops 11796480 | bytes 10487840 | tf_op jit(solution)/shard_map/convert_element_type | solution.py:150
  192.5 1.7 copy.45
  (87 shorter events, 16.6 us)
Async XLA Ops:
  13.1 27.0 %collective-permute-start.1 = (bf16[4,1,80,256]{3,0,2,1:T(4,128)(2,1)}, bf16[4,1,80,256]{3,0,2,1:T(4,128)(2,1)}, u32[]{:S(2)}, u32[]{:S(2)}) collective-permute-start(bf16[4,1,80,256]{3,0,2,1:T(4,128)(2,1)} %slice.155), channel_id=1, source_target_pairs={{0,8},{8,16},{16,24},{1,9},{9,17},{17,25},{2,10},{10,18},{18,26},{... | collective-permute-start | bytes 491528 | tf_op jit(solution)/shard_map/ppermute | solution.py:22
  17.9 23.6 %collective-permute-start.2 = (bf16[4,1,80,256]{3,0,2,1:T(4,128)(2,1)}, bf16[4,1,80,256]{3,0,2,1:T(4,128)(2,1)}, u32[]{:S(2)}, u32[]{:S(2)}) collective-permute-start(bf16[4,1,80,256]{3,0,2,1:T(4,128)(2,1)} %slice.159), channel_id=1, source_target_pairs={{8,0},{16,8},{24,16},{9,1},{17,9},{25,17},{10,2},{18,10},{26,18},{... | collective-permute-start | bytes 491528 | tf_op jit(solution)/shard_map/ppermute | solution.py:24
  20.4 22.7 %collective-permute-start.3 = (bf16[1,4,80,256]{3,0,2,1:T(2,128)(2,1)}, bf16[1,4,80,256]{3,0,2,1:T(2,128)(2,1)}, u32[]{:S(2)}, u32[]{:S(2)}) collective-permute-start(bf16[1,4,80,256]{3,0,2,1:T(2,128)(2,1)} %copy.30), channel_id=1, source_target_pairs={{0,1},{1,2},{2,3},{3,4},{4,5},{5,6},{6,7},{7,0},{8,9},{9,10},{10,1... | collective-permute-start | bytes 491528 | tf_op jit(solution)/shard_map/ppermute | solution.py:22
  23.8 21.0 %collective-permute-start.4 = (bf16[1,4,80,256]{3,0,2,1:T(2,128)(2,1)}, bf16[1,4,80,256]{3,0,2,1:T(2,128)(2,1)}, u32[]{:S(2)}, u32[]{:S(2)}) collective-permute-start(bf16[1,4,80,256]{3,0,2,1:T(2,128)(2,1)} %copy.34), channel_id=1, source_target_pairs={{1,0},{2,1},{3,2},{4,3},{5,4},{6,5},{7,6},{0,7},{9,8},{10,9},{11,1... | collective-permute-start | bytes 491528 | tf_op jit(solution)/shard_map/ppermute | solution.py:24
  28.2 2.8 %copy-start.19 = (bf16[4,4,80,320]{3,2,1,0:T(8,128)(2,1)S(1)}, bf16[4,4,80,320]{3,2,1,0:T(8,128)(2,1)}, u32[]{:S(2)}) copy-start(bf16[4,4,80,320]{3,2,1,0:T(8,128)(2,1)} %param.13) | copy-start | bytes 2457604
  30.9 25.7 %copy-start.10 = (bf16[4,4,80,320]{3,2,0,1:T(8,128)(2,1)}, bf16[4,4,80,320]{3,2,0,1:T(8,128)(2,1)S(1)}, u32[]{:S(2)}) copy-start(bf16[4,4,80,320]{3,2,0,1:T(8,128)(2,1)S(1)} %copy_bitcast_fusion) | copy-start | bytes 2457604
  31.4 3.7 %copy-start.15 = (bf16[3,4,5,1,4,4,256]{6,5,4,3,2,0,1:T(4,128)(2,1)S(1)}, bf16[3,4,5,1,4,4,256]{6,5,4,3,2,0,1:T(4,128)(2,1)}, u32[]{:S(2)}) copy-start(bf16[3,4,5,1,4,4,256]{6,5,4,3,2,0,1:T(4,128)(2,1)} %get-tuple-element.44) | copy-start | bytes 1474564
  32.2 4.2 %copy-start.16 = (f32[4,80,80]{2,1,0:T(8,128)}, f32[4,80,80]{2,1,0:T(8,128)S(1)}, u32[]{:S(2)}) copy-start(f32[4,80,80]{2,1,0:T(8,128)S(1)} %fusion.61) | copy-start | bytes 307204
  32.5 5.2 %copy-start.17 = (f32[4,80,80]{2,1,0:T(8,128)}, f32[4,80,80]{2,1,0:T(8,128)S(1)}, u32[]{:S(2)}) copy-start(f32[4,80,80]{2,1,0:T(8,128)S(1)} %fusion.78) | copy-start | bytes 307204
  32.5 5.2 %copy-start.13 = (bf16[4,4,5,4,1,4,256]{6,5,4,3,2,0,1:T(4,128)(2,1)S(1)}, bf16[4,4,5,4,1,4,256]{6,5,4,3,2,0,1:T(4,128)(2,1)}, u32[]{:S(2)}) copy-start(bf16[4,4,5,4,1,4,256]{6,5,4,3,2,0,1:T(4,128)(2,1)} %get-tuple-element.42) | copy-start | bytes 1966084
  32.8 6.1 %copy-start.18 = (f32[4,80,80]{2,1,0:T(8,128)}, f32[4,80,80]{2,1,0:T(8,128)S(1)}, u32[]{:S(2)}) copy-start(f32[4,80,80]{2,1,0:T(8,128)S(1)} %fusion.79) | copy-start | bytes 307204
  38.9 4.1 %copy-start.14 = (bf16[3,4,5,1,4,4,256]{6,0,5,4,2,1,3:T(4,128)(2,1)S(1)}, bf16[3,4,5,1,4,4,256]{6,0,5,4,2,1,3:T(4,128)(2,1)}, u32[]{:S(2)}) copy-start(bf16[3,4,5,1,4,4,256]{6,0,5,4,2,1,3:T(4,128)(2,1)} %copy.31) | copy-start | bytes 1474564
  41.5 5.0 %copy-start.21 = (bf16[4,4,5,4,1,4,256]{6,0,5,3,2,1,4:T(4,128)(2,1)S(1)}, bf16[4,4,5,4,1,4,256]{6,0,5,3,2,1,4:T(4,128)(2,1)}, u32[]{:S(2)}) copy-start(bf16[4,4,5,4,1,4,256]{6,0,5,3,2,1,4:T(4,128)(2,1)} %copy.35) | copy-start | bytes 1966084
  41.5 5.0 %copy-start.23 = (s32[1,4]{1,0:T(1,128)S(1)}, s32[1,4]{1,0:T(1,128)}, u32[]{:S(2)}) copy-start(s32[1,4]{1,0:T(1,128)} %param.10) | copy-start | bytes 52
  43.0 4.4 %copy-start.22 = (bf16[4,4,5,4,1,4,256]{6,0,5,3,2,1,4:T(4,128)(2,1)S(1)}, bf16[4,4,5,4,1,4,256]{6,0,5,3,2,1,4:T(4,128)(2,1)}, u32[]{:S(2)}) copy-start(bf16[4,4,5,4,1,4,256]{6,0,5,3,2,1,4:T(4,128)(2,1)} %copy.37) | copy-start | bytes 1966084
  48.1 4.8 %copy-start.1 = (bf16[4,4,320,256]{3,2,0,1:T(8,128)(2,1)S(1)}, bf16[4,4,320,256]{3,2,0,1:T(8,128)(2,1)}, u32[]{:S(2)}) copy-start(bf16[4,4,320,256]{3,2,0,1:T(8,128)(2,1)} %copy_multiply_fusion) | copy-start | bytes 7864324
  56.6 1.2 copy-start.20
  58.7 2.5 %copy-start.11 = (bf16[4,4,80,320]{3,2,0,1:T(8,128)(2,1)S(1)}, bf16[4,4,80,320]{3,2,0,1:T(8,128)(2,1)}, u32[]{:S(2)}) copy-start(bf16[4,4,80,320]{3,2,0,1:T(8,128)(2,1)} %copy-done.10) | copy-start | bytes 2457604
  62.0 1.1 copy-start.8
  63.9 1.1 copy-start.6
  66.8 4.8 %collective-permute-start = (f32[4,80,256]{2,1,0:T(8,128)}, f32[4,80,256]{2,1,0:T(8,128)S(1)}, u32[]{:S(2)}, u32[]{:S(2)}) collective-permute-start(f32[4,80,256]{2,1,0:T(8,128)} %convolution_add_fusion.2), channel_id=1, source_target_pairs={{0,8},{8,16},{16,24},{1,9},{9,17},{17,25},{2,10},{10,18},{18,26},{... | collective-permute-start | bytes 983048 | tf_op jit(solution)/shard_map/while/body/eval_jaxpr/ppermute | solution.py:34
  72.8 8.4 %collective-permute-start = (f32[4,80,256]{2,1,0:T(8,128)}, f32[4,80,256]{2,1,0:T(8,128)S(1)}, u32[]{:S(2)}, u32[]{:S(2)}) collective-permute-start(f32[4,80,256]{2,1,0:T(8,128)} %convolution_add_fusion.2), channel_id=1, source_target_pairs={{0,8},{8,16},{16,24},{1,9},{9,17},{17,25},{2,10},{10,18},{18,26},{... | collective-permute-start | bytes 983048 | tf_op jit(solution)/shard_map/while/body/eval_jaxpr/ppermute | solution.py:34
  82.4 8.6 %collective-permute-start = (f32[4,80,256]{2,1,0:T(8,128)}, f32[4,80,256]{2,1,0:T(8,128)S(1)}, u32[]{:S(2)}, u32[]{:S(2)}) collective-permute-start(f32[4,80,256]{2,1,0:T(8,128)} %convolution_add_fusion.2), channel_id=1, source_target_pairs={{0,8},{8,16},{16,24},{1,9},{9,17},{17,25},{2,10},{10,18},{18,26},{... | collective-permute-start | bytes 983048 | tf_op jit(solution)/shard_map/while/body/eval_jaxpr/ppermute | solution.py:34
  91.0 4.4 %copy-start.12 = (bf16[4,4,80,320]{3,2,0,1:T(8,128)(2,1)S(1)}, bf16[4,4,80,320]{3,2,0,1:T(8,128)(2,1)}, u32[]{:S(2)}) copy-start(bf16[4,4,80,320]{3,2,0,1:T(8,128)(2,1)} %copy-done.10) | copy-start | bytes 2457604
  95.4 1.6 copy-start.9
  96.2 2.8 %copy-start.2 = (f32[4,1,320,256]{3,2,0,1:T(8,128)}, f32[4,1,320,256]{3,2,0,1:T(8,128)S(1)}, u32[]{:S(2)}) copy-start(f32[4,1,320,256]{3,2,0,1:T(8,128)S(1)} %fusion.16) | copy-start | bytes 3932164
  96.2 2.0 %copy-start.7 = (f32[4,320,256]{2,1,0:T(8,128)S(1)}, f32[4,320,256]{2,1,0:T(8,128)}, u32[]{:S(2)}) copy-start(f32[4,320,256]{2,1,0:T(8,128)} %copy-done.6) | copy-start | bytes 3932164
  97.0 2.0 %copy-start.3 = (f32[4,1,320,256]{3,2,0,1:T(8,128)}, f32[4,1,320,256]{3,2,0,1:T(8,128)S(1)}, u32[]{:S(2)}) copy-start(f32[4,1,320,256]{3,2,0,1:T(8,128)S(1)} %fusion.18) | copy-start | bytes 3932164
  97.0 2.6 %copy-start = (bf16[4,4,320,256]{3,2,1,0:T(8,128)(2,1)S(1)}, bf16[4,4,320,256]{3,2,1,0:T(8,128)(2,1)}, u32[]{:S(2)}) copy-start(bf16[4,4,320,256]{3,2,1,0:T(8,128)(2,1)} %param.8) | copy-start | bytes 7864324
  98.2 2.9 %copy-start.4 = (f32[4,1,320,256]{3,2,0,1:T(8,128)}, f32[4,1,320,256]{3,2,0,1:T(8,128)S(1)}, u32[]{:S(2)}) copy-start(f32[4,1,320,256]{3,2,0,1:T(8,128)S(1)} %fusion.20) | copy-start | bytes 3932164
  99.6 1.6 copy-start.5
where the time goes:
time: 196 us; the launch traced here: 195 us
  blocking collectives  85.1 us (43%)
  matrix products  29.9 us (15%)
  local copies, waits for them, and re-layouts  28.1 us (14%)
  starting transfers between devices  27.2 us (14%)
  other arithmetic  18.8 us (10%)
  waiting for transfers between devices  4.28 us (2%)
    psum x1, blocking collectives, per_device(): lax.psum((jnp.sum(masked_wide * eliminated, axis=(0, 1, 2)), jnp.sum(mask...  43.8 us
    psum x1, blocking collectives, per_device(): lax.psum(jnp.sum(remainder * remainder, axis=(0, 1, 2)), ('wall', 'surf'))  41.3 us
    dot_general x27, matrix products, exact_times(): jnp.einsum(form, left.astype(jnp.float32), right.astype(jnp.float32), pre...  19.8 us
    ppermute x3, starting transfers between devices, from_behind(): return lax.ppermute(shard, axis, pairs)  17.6 us
    unnamed x4, other arithmetic  6.28 us
    ppermute x2, starting transfers between devices, with_halo(): lax.ppermute(tail, axis, [(i, (i + 1) % count) for i in range(ends)])  5.37 us
    unnamed x51, local copies, waits for them, and re-layouts  4.98 us
    dot_general x1, matrix products, per_device(): jnp.einsum('lsgfb,lsgfr->lsbr', lifting, neighbours, preferred_element_ty...  4.77 us
  transfers between devices with their start and end apart: 7, of which 3 were waited for; matrix products, arithmetic and copies ran while one was open for 11% of the time, Pallas kernels for 0%

commit v1 on v0

v1 whole, which is shorter than its diff:
```python
import functools

import jax
import jax.numpy as jnp
from jax import lax
from jax.experimental import pallas as pl
from jax.experimental.pallas import tpu as pltpu
from jax.sharding import PartitionSpec as P

NODE1D = 4
F32 = jnp.float32
BF16 = jnp.bfloat16
MESH = pl.DeviceIdType.MESH


def times(a, b):
    return lax.dot_general(a, b, (((1,), (0,)), ((), ())), preferred_element_type=F32)


def left_t(a, b):
    return lax.dot_general(a, b, (((0,), (0,)), ((), ())), preferred_element_type=F32)


def right_t(a, b):
    return lax.dot_general(a, b, (((1,), (1,)), ((), ())), preferred_element_type=F32)


def split(x):
    high = x.astype(BF16)
    return high, (x - high.astype(F32)).astype(BF16)


def selector(face, block):
    entry = lax.broadcasted_iota(jnp.int32, (face, block), 0)
    column = lax.broadcasted_iota(jnp.int32, (face, block), 1)
    last = NODE1D - 1
    along = NODE1D * entry
    across = NODE1D * NODE1D * (entry // NODE1D) + entry % NODE1D
    wanted = (along + last, along, across, across + last * NODE1D)
    return [jnp.where(column == at, 1.0, 0.0).astype(BF16) for at in wanted]


def merge(gathered, count):
    p = [gathered[i, 0:1] for i in range(count)]
    s = [gathered[i, 1:2] for i in range(count)]
    o = [gathered[i, 2:3] for i in range(count)]
    r = [gathered[i, 3:4] for i in range(count)]
    total = sum(s[1:], s[0])
    cross = sum((o[i] + p[i] * s[i] for i in range(1, count)), o[0] + p[0] * s[0])
    safe = jnp.where(total > 0.0, total, 1.0)
    common = jnp.where(total > 0.0, cross / safe, 0.0)
    odd = jnp.zeros_like(total)
    square = jnp.zeros_like(total)
    for i in range(count):
        shift = p[i] - common
        odd = odd + (o[i] + shift * s[i])
        square = square + (r[i] + shift * (2.0 * o[i] + shift * s[i]))
    return common, total, odd, square, cross


def kernel(
    sizes, lengths, north_of, vector, diagonal, lifting, inverse, basis, coefs,
    xv, dg, lf, iv, sel, top, bottom, west, east, south, north,
    below_in, above_in, west_in, east_in, prod, carry, carry_f, gt, q, mt, cin, cout,
    stat1, all1, stat2, all2,
    in_sem, halo_send, halo_recv, chain_send, chain_recv, s1_send, s1_recv, s2_send, s2_recv,
):
    lines, seg, block, face, cols, walls, surfs = sizes
    w = lax.axis_index("wall")
    s = lax.axis_index("surf")
    loads = []
    for n, (src, dst) in enumerate(((vector, xv), (diagonal, dg), (lifting, lf), (inverse, iv))):
        for l in range(lines):
            loads.append(pltpu.make_async_copy(src.at[l], dst.at[l], in_sem.at[n, l]))
    for copy in loads:
        copy.start()
    barrier = pltpu.get_barrier_semaphore()
    for d in range(1, walls):
        pl.semaphore_signal(
            barrier, inc=1, device_id={"wall": lax.rem(w + d, walls)}, device_id_type=MESH
        )
    for d in range(1, surfs):
        pl.semaphore_signal(
            barrier, inc=1, device_id={"surf": lax.rem(s + d, surfs)}, device_id_type=MESH
        )

    def alive(l, k):
        return jnp.where(w * seg + k < lengths[l], 1.0, 0.0).astype(F32)

    def element(i):
        return i // seg, i % seg

    for g, rows in enumerate(selector(face, block)):
        sel[g * face:(g + 1) * face] = rows
    plane = NODE1D * NODE1D
    cube = plane * NODE1D

    for copy in loads[:lines]:
        copy.wait()

    def mask_one(i, _):
        l, k = element(i)
        x = (xv[l, k].astype(F32) * alive(l, k)).astype(BF16)
        xv[l, k] = x
        west[l, k] = jnp.concatenate([x[v:v + plane] for v in range(0, block, cube)], axis=0)
        east[l + 1, k] = jnp.concatenate(
            [x[v + cube - plane:v + cube] for v in range(0, block, cube)], axis=0
        )
        return 0

    lax.fori_loop(0, lines * seg, mask_one, 0)
    pl.semaphore_wait(barrier, walls - 1 + surfs - 1)

    def remote(src, dst, send, recv, target):
        return pltpu.make_async_remote_copy(
            src_ref=src, dst_ref=dst, send_sem=send, recv_sem=recv,
            device_id=target, device_id_type=MESH,
        )

    to_east = remote(
        east.at[lines], west_in, halo_send.at[0], halo_recv.at[0],
        {"surf": lax.rem(s + 1, surfs)},
    )
    to_west = remote(
        west.at[0], east_in, halo_send.at[1], halo_recv.at[1],
        {"surf": lax.rem(s + surfs - 1, surfs)},
    )
    to_east.start()
    to_west.start()

    def trace_one(i, _):
        l, k = element(i)
        t = times(sel[...], xv[l, k]).astype(BF16)
        top[l, k + 1] = t[:face]
        bottom[l, k] = t[face:2 * face]
        south[l, k] = t[2 * face:3 * face]
        north[l, k] = t[3 * face:]
        return 0

    lax.fori_loop(0, lines * seg, trace_one, 0)

    up = {"wall": lax.rem(w + 1, walls)}
    down = {"wall": lax.rem(w + walls - 1, walls)}
    to_above = remote(top.at[:, seg], below_in, halo_send.at[2], halo_recv.at[2], up)
    to_below = remote(bottom.at[:, 0], above_in, halo_send.at[3], halo_recv.at[3], down)

    @pl.when(w < walls - 1)
    def _():
        to_above.start()

    @pl.when(w > 0)
    def _():
        to_below.start()

    for copy in loads[lines:]:
        copy.wait()

    def local_one(i, _):
        l, k = element(i)
        south_line = jnp.int32(0)
        for j in range(lines):
            south_line = jnp.where(north_of[0, j] == l, j, south_line)
        sides = jnp.concatenate([north[south_line, k], south[north_of[0, l], k]], axis=0)
        prod[l, k] = times(dg[l, k], xv[l, k]) + left_t(lf[l, k, 4 * face:6 * face], sides)
        return 0

    lax.fori_loop(0, lines * seg, local_one, 0)

    row = lax.broadcasted_iota(jnp.int32, (face, face), 0)
    column = lax.broadcasted_iota(jnp.int32, (face, face), 1)
    eye = jnp.where(row == column, 1.0, 0.0).astype(F32)
    for l in range(lines):
        q[l] = eye

    def map_step(k, _):
        for l in range(lines):
            qh, ql = split(q[l])
            lower = lf[l, k, 0:face]
            g = alive(l, k) * (times(qh, lower) + times(ql, lower))
            gh, gl = split(g)
            gt[l, k, 0:face] = gh
            gt[l, k, face:2 * face] = gl
            gt[l, k, 2 * face:3 * face] = gh
            q[l] = -(right_t(gh, iv[l, k]) + right_t(gl, iv[l, k]))
        return 0

    lax.fori_loop(0, seg, map_step, 0)
    for l in range(lines):
        mh, ml = split(q[l])
        mt[l, 0:face] = mh
        mt[l, face:2 * face] = ml
        mt[l, 2 * face:3 * face] = mh

    carry[...] = jnp.zeros_like(carry)

    @pl.when(w > 0)
    def _():
        to_above.wait_recv()
        for l in range(lines):
            top[l, 0] = below_in[l]

    @pl.when(w == 0)
    def _():
        for l in range(lines):
            top[l, 0] = jnp.zeros((face, cols), BF16)

    @pl.when(w < walls - 1)
    def _():
        to_below.wait_recv()
        for l in range(lines):
            bottom[l, seg] = above_in[l]

    @pl.when(w == walls - 1)
    def _():
        for l in range(lines):
            bottom[l, seg] = jnp.zeros((face, cols), BF16)

    to_east.wait_recv()
    east[0] = west_in[...]
    to_west.wait_recv()
    west[lines] = east_in[...]

    def free_step(k, _):
        for l in range(lines):
            blocks = jnp.concatenate(
                [lf[l, k, 0:4 * face], lf[l, k, 0:face], lf[l, k, 0:face]], axis=0
            )
            sides = jnp.concatenate(
                [top[l, k], bottom[l, k + 1], east[l, k], west[l + 1, k], carry[l]], axis=0
            )
            e = alive(l, k) * (prod[l, k] + left_t(blocks, sides))
            prod[l, k] = e
            eh, el = split(e)
            c = times(iv[l, k], eh) + times(iv[l, k], el)
            carry_f[l] = c
            ch, cl = split(-c)
            carry[l, 0:face] = ch
            carry[l, face:2 * face] = cl
        return 0

    lax.fori_loop(0, seg, free_step, 0)

    chain = [
        remote(cout.at[l], cin.at[l], chain_send.at[l], chain_recv.at[l], up)
        for l in range(lines)
    ]

    @pl.when(w == 0)
    def _():
        for l in range(lines):
            cout[l] = carry_f[l]
            chain[l].start()

    def first_sums(i, acc):
        l, k = element(i)
        x = xv[l, k].astype(F32)
        e = prod[l, k]
        xs = x.reshape(block // 8, 8, cols)
        es = e.reshape(block // 8, 8, cols)
        return acc[0] + jnp.sum(xs * es, axis=0), acc[1] + jnp.sum(xs * xs, axis=0)

    nothing = jnp.zeros((8, cols), F32)
    near, norm = lax.fori_loop(0, lines * seg, first_sums, (nothing, nothing))
    near = jnp.sum(near, axis=0, keepdims=True)
    norm = jnp.sum(norm, axis=0, keepdims=True)
    guess = jnp.where(norm > 0.0, near / jnp.where(norm > 0.0, norm, 1.0), 0.0)

    def packed(l):
        high, low = split(cin[l])
        return jnp.concatenate([high, high, low], axis=0)

    @pl.when(w > 0)
    def _():
        for l in range(lines):
            chain[l].wait_recv()

            @pl.when(w < walls - 1)
            def _():
                cout[l] = carry_f[l] + left_t(mt[l], packed(l))
                chain[l].start()

        def correct(i, _):
            l, k = element(i)
            prod[l, k] = prod[l, k] - left_t(gt[l, k], packed(l))
            return 0

        lax.fori_loop(0, lines * seg, correct, 0)

    def second_sums(i, acc):
        l, k = element(i)
        x = xv[l, k].astype(F32)
        e = prod[l, k] - guess * x
        xs = x.reshape(block // 8, 8, cols)
        es = e.reshape(block // 8, 8, cols)
        return acc[0] + jnp.sum(xs * es, axis=0), acc[1] + jnp.sum(es * es, axis=0)

    odd, square = lax.fori_loop(0, lines * seg, second_sums, (nothing, nothing))
    odd = jnp.sum(odd, axis=0, keepdims=True)
    square = jnp.sum(square, axis=0, keepdims=True)

    def gather(values, stat, slots, sends, recvs, axis, me, count):
        block_of = jnp.concatenate(list(values) + [jnp.zeros((4, cols), F32)], axis=0)
        stat[...] = block_of
        slots[me] = block_of
        copies = [
            remote(
                stat, slots.at[me], sends.at[d], recvs.at[d], {axis: lax.rem(me + d, count)}
            )
            for d in range(1, count)
        ]
        for copy in copies:
            copy.start()
        for copy in copies:
            copy.wait_recv()
        return copies

    sent1 = gather((guess, norm, odd, square), stat1, all1, s1_send, s1_recv, "wall", w, walls)
    common, total, odd, square, _ = merge(all1, walls)
    sent2 = gather((common, total, odd, square), stat2, all2, s2_send, s2_recv, "surf", s, surfs)
    _, total, _, square, cross = merge(all2, surfs)
    projection = cross / total
    entries = lines * seg * block * walls * surfs
    spread = jnp.sqrt(square / entries + 1e-06)
    coefs[0:1] = projection
    coefs[1:2] = spread
    scale = 1.0 / spread

    def finish(i, _):
        l, k = element(i)
        basis[l, k] = ((prod[l, k] - projection * xv[l, k].astype(F32)) * scale).astype(BF16)
        return 0

    lax.fori_loop(0, lines * seg, finish, 0)

    for copy in sent1 + sent2 + [to_east, to_west]:
        copy.wait_send()

    @pl.when(w < walls - 1)
    def _():
        to_above.wait_send()
        for copy in chain:
            copy.wait_send()

    @pl.when(w > 0)
    def _():
        to_below.wait_send()


def per_device(walls, surfs, vector, lengths, north_of, diagonal, lifting, inverse_rows):
    lines, seg, block, cols = vector.shape
    face = inverse_rows.shape[2]
    sizes = (lines, seg, block, face, cols, walls, surfs)
    stacked = lifting.reshape(lines, seg, lifting.shape[2] * face, block)
    smem = pl.BlockSpec(memory_space=pltpu.SMEM)
    vmem = pl.BlockSpec(memory_space=pltpu.VMEM)
    hbm = pl.BlockSpec(memory_space=pl.ANY)
    dma = pltpu.SemaphoreType.DMA
    return pl.pallas_call(
        functools.partial(kernel, sizes),
        out_shape=(
            jax.ShapeDtypeStruct(vector.shape, BF16),
            jax.ShapeDtypeStruct((2, cols), F32),
        ),
        in_specs=[smem, smem, hbm, hbm, hbm, hbm],
        out_specs=(vmem, vmem),
        scratch_shapes=[
            pltpu.VMEM(vector.shape, BF16),
            pltpu.VMEM(diagonal.shape, BF16),
            pltpu.VMEM(stacked.shape, BF16),
            pltpu.VMEM(inverse_rows.shape, BF16),
            pltpu.VMEM((4 * face, block), BF16),
            pltpu.VMEM((lines, seg + 1, face, cols), BF16),
            pltpu.VMEM((lines, seg + 1, face, cols), BF16),
            pltpu.VMEM((lines + 1, seg, face, cols), BF16),
            pltpu.VMEM((lines + 1, seg, face, cols), BF16),
            pltpu.VMEM((lines, seg, face, cols), BF16),
            pltpu.VMEM((lines, seg, face, cols), BF16),
            pltpu.VMEM((lines, face, cols), BF16),
            pltpu.VMEM((lines, face, cols), BF16),
            pltpu.VMEM((seg, face, cols), BF16),
            pltpu.VMEM((seg, face, cols), BF16),
            pltpu.VMEM(vector.shape, F32),
            pltpu.VMEM((lines, 2 * face, cols), BF16),
            pltpu.VMEM((lines, face, cols), F32),
            pltpu.VMEM((lines, seg, 3 * face, block), BF16),
            pltpu.VMEM((lines, face, face), F32),
            pltpu.VMEM((lines, 3 * face, face), BF16),
            pltpu.VMEM((lines, face, cols), F32),
            pltpu.VMEM((lines, face, cols), F32),
            pltpu.VMEM((8, cols), F32),
            pltpu.VMEM((walls, 8, cols), F32),
            pltpu.VMEM((8, cols), F32),
            pltpu.VMEM((surfs, 8, cols), F32),
            dma((4, lines)),
            dma((4,)),
            dma((4,)),
            dma((lines,)),
            dma((lines,)),
            dma((walls,)),
            dma((walls,)),
            dma((surfs,)),
            dma((surfs,)),
        ],
        compiler_params=pltpu.CompilerParams(
            collective_id=0, has_side_effects=True, vmem_limit_bytes=60 * 1024 * 1024
        ),
    )(lengths, north_of, vector, diagonal, stacked, inverse_rows)


def solution(mesh):
    in_specs = (
        P("surf", "wall", None, None),
        P("surf"),
        P("surf", None),
        P("surf", "wall", None, None),
        P("surf", "wall", None, None, None),
        P("surf", "wall", None, None),
    )
    out_specs = (P("surf", "wall", None, None), P())
    return jax.shard_map(
        functools.partial(per_device, mesh.shape["wall"], mesh.shape["surf"]),
        mesh=mesh, in_specs=in_specs, out_specs=out_specs, check_vma=False,
    )
```

time: 196 us -> 53.5 us (0.27)
  blocking collectives: 85.1 us -> 0 us
  Pallas kernels: 0 us -> 48.6 us
  matrix products: 29.9 us -> 0 us
  starting transfers between devices: 27.2 us -> 0 us
  local copies, waits for them, and re-layouts: 28.1 us -> 4.05 us
  other arithmetic: 18.8 us -> 0 us
  waiting for transfers between devices: 4.28 us -> 0 us
    psum x2 -> x0, blocking collectives: 85.1 us -> none  [the longest x1 43.8 us: per_device(): lax.psum((jnp.sum(masked_wide * eliminated, axis=(0, 1, 2)), jnp.sum(mask...]
    pallas_call x0 -> x1, Pallas kernels: none -> 48.6 us  [per_device(): pl.pallas_call(functools.partial(kernel, sizes), out_shape=(jax.ShapeDtyp...]
    dot_general x31 -> x0, matrix products: 29.9 us -> none  [the longest x27 19.8 us: exact_times(): jnp.einsum(form, left.astype(jnp.float32), right.astype(jnp.float32), pre...]
    ppermute x7 -> x0, starting transfers between devices: 27.2 us -> none  [the longest x3 17.6 us: from_behind(): return lax.ppermute(shard, axis, pairs)]
    slice x16 -> x0, local copies, waits for them, and re-layouts: 18.1 us -> none  [the longest x2 3.96 us: face_traces(): bottom_face = flatten(nodal_cube[..., 0, :])]
    unnamed x4 -> x0, other arithmetic: 6.28 us -> none
    reduce_sum x2 -> x0, other arithmetic: 4.69 us -> none  [the longest x1 3.13 us: per_device(): jnp.sum(remainder * remainder, axis=(0, 1, 2))]
    ppermute x7 -> x0, waiting for transfers between devices: 4.28 us -> none  [the longest x3 4.27 us: from_behind(): return lax.ppermute(shard, axis, pairs)]
  transfers between devices with their start and end apart: 7 -> 0, of which waited for: 3 -> 0; matrix products, arithmetic and copies ran while one was open for 11% -> 0% of each run, Pallas kernels for 0% -> 0%
where the time goes in v1:
time: 53.5 us; the launch traced here: 53.3 us
  Pallas kernels  48.6 us (91%)
  local copies, waits for them, and re-layouts  4.05 us (8%)
  between operations  0.65 us (1%)
    pallas_call x1, Pallas kernels, per_device(): pl.pallas_call(functools.partial(kernel, sizes), out_shape=(jax.ShapeDtyp...  48.6 us
    unnamed x4, local copies, waits for them, and re-layouts  4.05 us

profile of v1, /device:TPU:0, one launch (start us, length us, event | category | flops | bytes accessed | tf_op | source)
XLA Modules:
  0.0 53.3 jit_solution(17448472170427414749)
XLA Ops:
  0.6 48.6 %shard_map.77 = (bf16[4,4,320,256]{3,2,1,0:T(8,128)(2,1)}, f32[2,256]{1,0:T(2,128)}) custom-call(s32[4]{0:T(128)} %lengths.1, s32[1,4]{1,0:T(1,128)} %north_of.1, bf16[4,4,320,256]{3,2,1,0:T(8,128)(2,1)} %vector.1, bf16[4,4,320,320]{3,2,1,0:T(8,128)(2,1)} %diagonal.1, bf16[4,4,480,320]{3,2,1,0:T(8,128)(2,1)} %bitcast.1, bf16[4,4,80,320]{3,2,1,0:T(8,128)(2,1)} %inverse.1), custom_call_target="tpu_custom_call" | custom-call | tf_op jit(solution)/shard_map/pallas_call | solution.py:358
  49.2 0.0 copy-start
  49.3 3.5 %copy.10 = bf16[4,4,320,256]{3,2,1,0:T(8,128)(2,1)} copy(bf16[4,4,320,256]{3,2,1,0:T(8,128)(2,1)} %get-tuple-element.4) | data formatting | bytes 5242880
  52.7 0.0 copy-done
  52.7 0.6 %copy.11 = f32[2,256]{1,0:T(2,128)} copy(f32[2,256]{1,0:T(2,128)S(1)} %copy-done) | data formatting | bytes 4096
Async XLA Ops:
  49.2 3.5 %copy-start = (f32[2,256]{1,0:T(2,128)S(1)}, f32[2,256]{1,0:T(2,128)}, u32[]{:S(2)}) copy-start(f32[2,256]{1,0:T(2,128)} %get-tuple-element.5) | copy-start | bytes 6148

commit v2 on v1

--- a/solution.py
+++ b/solution.py
@@ -59,9 +59,9 @@
 
 
 def kernel(
-    sizes, lengths, north_of, vector, diagonal, lifting, inverse, basis, coefs,
-    xv, dg, lf, iv, sel, top, bottom, west, east, south, north,
-    below_in, above_in, west_in, east_in, prod, carry, carry_f, gt, q, mt, cin, cout,
+    sizes, lengths, north_of, vector, diagonal, lifting, inverse, xv, prod, coefs,
+    dg, lf, iv, sel, top, bottom, west, east, south, north,
+    below_in, above_in, west_in, east_in, carry, carry_f, gt, q, mt, cin, cpack, cout,
     stat1, all1, stat2, all2,
     in_sem, halo_send, halo_recv, chain_send, chain_recv, s1_send, s1_recv, s2_send, s2_recv,
 ):
@@ -137,7 +137,7 @@
         north[l, k] = t[3 * face:]
         return 0
 
-    lax.fori_loop(0, lines * seg, trace_one, 0)
+    lax.fori_loop(0, lines * seg, trace_one, 0, unroll=2)
 
     up = {"wall": lax.rem(w + 1, walls)}
     down = {"wall": lax.rem(w + walls - 1, walls)}
@@ -164,7 +164,7 @@
         prod[l, k] = times(dg[l, k], xv[l, k]) + left_t(lf[l, k, 4 * face:6 * face], sides)
         return 0
 
-    lax.fori_loop(0, lines * seg, local_one, 0)
+    lax.fori_loop(0, lines * seg, local_one, 0, unroll=2)
 
     row = lax.broadcasted_iota(jnp.int32, (face, face), 0)
     column = lax.broadcasted_iota(jnp.int32, (face, face), 1)
@@ -265,36 +265,33 @@
     norm = jnp.sum(norm, axis=0, keepdims=True)
     guess = jnp.where(norm > 0.0, near / jnp.where(norm > 0.0, norm, 1.0), 0.0)
 
-    def packed(l):
-        high, low = split(cin[l])
-        return jnp.concatenate([high, high, low], axis=0)
+    @pl.when(w == 0)
+    def _():
+        cpack[...] = jnp.zeros_like(cpack)
 
     @pl.when(w > 0)
     def _():
         for l in range(lines):
             chain[l].wait_recv()
+            high, low = split(cin[l])
+            cpack[l] = jnp.concatenate([high, high, low], axis=0)
 
             @pl.when(w < walls - 1)
             def _():
-                cout[l] = carry_f[l] + left_t(mt[l], packed(l))
+                cout[l] = carry_f[l] + left_t(mt[l], cpack[l])
                 chain[l].start()
 
-        def correct(i, _):
-            l, k = element(i)
-            prod[l, k] = prod[l, k] - left_t(gt[l, k], packed(l))
-            return 0
-
-        lax.fori_loop(0, lines * seg, correct, 0)
-
-    def second_sums(i, acc):
+    def correct(i, acc):
         l, k = element(i)
+        e = prod[l, k] - left_t(gt[l, k], cpack[l])
+        prod[l, k] = e
         x = xv[l, k].astype(F32)
-        e = prod[l, k] - guess * x
+        e = e - guess * x
         xs = x.reshape(block // 8, 8, cols)
         es = e.reshape(block // 8, 8, cols)
         return acc[0] + jnp.sum(xs * es, axis=0), acc[1] + jnp.sum(es * es, axis=0)
 
-    odd, square = lax.fori_loop(0, lines * seg, second_sums, (nothing, nothing))
+    odd, square = lax.fori_loop(0, lines * seg, correct, (nothing, nothing), unroll=2)
     odd = jnp.sum(odd, axis=0, keepdims=True)
     square = jnp.sum(square, axis=0, keepdims=True)
 
@@ -323,15 +320,6 @@
     spread = jnp.sqrt(square / entries + 1e-06)
     coefs[0:1] = projection
     coefs[1:2] = spread
-    scale = 1.0 / spread
-
-    def finish(i, _):
-        l, k = element(i)
-        basis[l, k] = ((prod[l, k] - projection * xv[l, k].astype(F32)) * scale).astype(BF16)
-        return 0
-
-    lax.fori_loop(0, lines * seg, finish, 0)
-
     for copy in sent1 + sent2 + [to_east, to_west]:
         copy.wait_send()
 
@@ -344,6 +332,16 @@
     @pl.when(w > 0)
     def _():
         to_below.wait_send()
+
+
+def finish(masked, eliminated, stats, basis, coefs):
+    l = pl.program_id(0)
+    coefs[...] = stats[...]
+    projection = stats[0:1]
+    scale = 1.0 / stats[1:2]
+    for k in range(basis.shape[1]):
+        x = masked[l, k].astype(F32)
+        basis[0, k] = ((eliminated[l, k] - projection * x) * scale).astype(BF16)
 
 
 def per_device(walls, surfs, vector, lengths, north_of, diagonal, lifting, inverse_rows):
@@ -353,18 +351,18 @@
     stacked = lifting.reshape(lines, seg, lifting.shape[2] * face, block)
     smem = pl.BlockSpec(memory_space=pltpu.SMEM)
     vmem = pl.BlockSpec(memory_space=pltpu.VMEM)
-    hbm = pl.BlockSpec(memory_space=pl.ANY)
+    hbm = pl.BlockSpec(memory_space=pltpu.HBM)
     dma = pltpu.SemaphoreType.DMA
-    return pl.pallas_call(
+    masked, eliminated, stats = pl.pallas_call(
         functools.partial(kernel, sizes),
         out_shape=(
-            jax.ShapeDtypeStruct(vector.shape, BF16),
-            jax.ShapeDtypeStruct((2, cols), F32),
+            pltpu.VMEM(vector.shape, BF16),
+            pltpu.VMEM(vector.shape, F32),
+            pltpu.VMEM((2, cols), F32),
         ),
         in_specs=[smem, smem, hbm, hbm, hbm, hbm],
-        out_specs=(vmem, vmem),
+        out_specs=(vmem, vmem, vmem),
         scratch_shapes=[
-            pltpu.VMEM(vector.shape, BF16),
             pltpu.VMEM(diagonal.shape, BF16),
             pltpu.VMEM(stacked.shape, BF16),
             pltpu.VMEM(inverse_rows.shape, BF16),
@@ -379,13 +377,13 @@
             pltpu.VMEM((lines, face, cols), BF16),
             pltpu.VMEM((seg, face, cols), BF16),
             pltpu.VMEM((seg, face, cols), BF16),
-            pltpu.VMEM(vector.shape, F32),
             pltpu.VMEM((lines, 2 * face, cols), BF16),
             pltpu.VMEM((lines, face, cols), F32),
             pltpu.VMEM((lines, seg, 3 * face, block), BF16),
             pltpu.VMEM((lines, face, face), F32),
             pltpu.VMEM((lines, 3 * face, face), BF16),
             pltpu.VMEM((lines, face, cols), F32),
+            pltpu.VMEM((lines, 3 * face, cols), BF16),
             pltpu.VMEM((lines, face, cols), F32),
             pltpu.VMEM((8, cols), F32),
             pltpu.VMEM((walls, 8, cols), F32),
@@ -402,9 +400,23 @@
             dma((surfs,)),
         ],
         compiler_params=pltpu.CompilerParams(
-            collective_id=0, has_side_effects=True, vmem_limit_bytes=60 * 1024 * 1024
+            collective_id=0, has_side_effects=True, vmem_limit_bytes=56 * 1024 * 1024
         ),
     )(lengths, north_of, vector, diagonal, stacked, inverse_rows)
+    return pl.pallas_call(
+        finish,
+        grid=(lines,),
+        out_shape=(
+            jax.ShapeDtypeStruct(vector.shape, BF16),
+            jax.ShapeDtypeStruct((2, cols), F32),
+        ),
+        in_specs=[vmem, vmem, vmem],
+        out_specs=(
+            pl.BlockSpec((1, seg, block, cols), lambda l: (l, 0, 0, 0)),
+            pl.BlockSpec((2, cols), lambda l: (0, 0)),
+        ),
+        compiler_params=pltpu.CompilerParams(vmem_limit_bytes=16 * 1024 * 1024),
+    )(masked, eliminated, stats)
 
 
 def solution(mesh):

time: 53.5 us -> 44.3 us (0.83)
  Pallas kernels: 48.6 us -> 43.5 us
  local copies, waits for them, and re-layouts: 4.05 us -> 0 us
    pallas_call x1 -> x2, Pallas kernels: 48.6 us -> 43.5 us  [the longest x1 41.2 us: per_device(): pl.pallas_call(functools.partial(kernel, sizes), out_shape=(pltpu.VMEM(ve...]
    unnamed x4 -> x0, local copies, waits for them, and re-layouts: 4.05 us -> none
where the time goes in v2:
time: 44.3 us; the launch traced here: 44.2 us
  Pallas kernels  43.5 us (98%)
  between operations  0.64 us (1%)
    pallas_call x1, Pallas kernels, per_device(): pl.pallas_call(functools.partial(kernel, sizes), out_shape=(pltpu.VMEM(ve...  41.2 us
    pallas_call x1, Pallas kernels, per_device(): pl.pallas_call(finish, grid=(lines,), out_shape=(jax.ShapeDtypeStruct(vec...  2.3 us

profile of v2, /device:TPU:0, one launch (start us, length us, event | category | flops | bytes accessed | tf_op | source)
XLA Modules:
  0.0 44.2 jit_solution(4421635302279282121)
XLA Ops:
  0.6 41.2 %shard_map.77 = (bf16[4,4,320,256]{3,2,1,0:T(8,128)(2,1)S(1)}, f32[4,4,320,256]{3,2,1,0:T(8,128)S(1)}, f32[2,256]{1,0:T(2,128)S(1)}) custom-call(s32[4]{0:T(128)} %lengths.1, s32[1,4]{1,0:T(1,128)} %north_of.1, bf16[4,4,320,256]{3,2,1,0:T(8,128)(2,1)} %vector.1, bf16[4,4,320,320]{3,2,1,0:T(8,128)(2,1)} %diagonal.1, bf16[4,4,480,320]{3,2,1,0:T(8,128)(2,1)} %bitcast.1, ...), custom_call_target="tpu_custom_call" | custom-call | tf_op jit(solution)/shard_map/pallas_call | solution.py:356
  41.9 2.3 %shard_map.78 = (bf16[4,4,320,256]{3,2,1,0:T(8,128)(2,1)}, f32[2,256]{1,0:T(2,128)}) custom-call(bf16[4,4,320,256]{3,2,1,0:T(8,128)(2,1)S(1)} %get-tuple-element.5.masked, f32[4,4,320,256]{3,2,1,0:T(8,128)S(1)} %get-tuple-element.6.eliminated, f32[2,256]{1,0:T(2,128)S(1)} %get-tuple-element.7.stats), custom_call_target="tpu_custom_call" | custom-call | tf_op jit(solution)/shard_map/pallas_call | solution.py:406

commit v3 on v2

--- a/solution.py
+++ b/solution.py
@@ -72,7 +72,8 @@
     for n, (src, dst) in enumerate(((vector, xv), (diagonal, dg), (lifting, lf), (inverse, iv))):
         for l in range(lines):
             loads.append(pltpu.make_async_copy(src.at[l], dst.at[l], in_sem.at[n, l]))
-    for copy in loads:
+    first = sorted(range(lines), key=lambda l: min(l, lines - 1 - l))
+    for copy in [loads[l] for l in first] + loads[lines:]:
         copy.start()
     barrier = pltpu.get_barrier_semaphore()
     for d in range(1, walls):
@@ -95,20 +96,26 @@
     plane = NODE1D * NODE1D
     cube = plane * NODE1D
 
-    for copy in loads[:lines]:
-        copy.wait()
-
-    def mask_one(i, _):
-        l, k = element(i)
+    def mask_one(l, k):
         x = (xv[l, k].astype(F32) * alive(l, k)).astype(BF16)
         xv[l, k] = x
         west[l, k] = jnp.concatenate([x[v:v + plane] for v in range(0, block, cube)], axis=0)
         east[l + 1, k] = jnp.concatenate(
             [x[v + cube - plane:v + cube] for v in range(0, block, cube)], axis=0
         )
-        return 0
-
-    lax.fori_loop(0, lines * seg, mask_one, 0)
+
+    def mask_line(l):
+        def one(k, _):
+            mask_one(l, k)
+            return 0
+
+        loads[l].wait()
+        lax.fori_loop(0, seg, one, 0)
+
+    outer = sorted({0, lines - 1})
+    inner = [l for l in range(lines) if l not in outer]
+    for l in outer:
+        mask_line(l)
     pl.semaphore_wait(barrier, walls - 1 + surfs - 1)
 
     def remote(src, dst, send, recv, target):
@@ -127,6 +134,8 @@
     )
     to_east.start()
     to_west.start()
+    for l in inner:
+        mask_line(l)
 
     def trace_one(i, _):
         l, k = element(i)
@@ -215,13 +224,8 @@
         for l in range(lines):
             bottom[l, seg] = jnp.zeros((face, cols), BF16)
 
-    to_east.wait_recv()
-    east[0] = west_in[...]
-    to_west.wait_recv()
-    west[lines] = east_in[...]
-
-    def free_step(k, _):
-        for l in range(lines):
+    def free_step(group, k, _):
+        for l in group:
             blocks = jnp.concatenate(
                 [lf[l, k, 0:4 * face], lf[l, k, 0:face], lf[l, k, 0:face]], axis=0
             )
@@ -238,18 +242,44 @@
             carry[l, face:2 * face] = cl
         return 0
 
-    lax.fori_loop(0, seg, free_step, 0)
-
     chain = [
         remote(cout.at[l], cin.at[l], chain_send.at[l], chain_recv.at[l], up)
         for l in range(lines)
     ]
 
-    @pl.when(w == 0)
-    def _():
-        for l in range(lines):
-            cout[l] = carry_f[l]
+    def begin(group):
+        @pl.when(w == 0)
+        def _():
+            for l in group:
+                cout[l] = carry_f[l]
+                chain[l].start()
+
+    def take(l):
+        chain[l].wait_recv()
+        high, low = split(cin[l])
+        cpack[l] = jnp.concatenate([high, high, low], axis=0)
+
+        @pl.when(w < walls - 1)
+        def _():
+            cout[l] = carry_f[l] + left_t(mt[l], cpack[l])
             chain[l].start()
+
+    lax.fori_loop(0, seg, functools.partial(free_step, inner), 0)
+    begin(inner)
+    to_east.wait_recv()
+    east[0] = west_in[...]
+    to_west.wait_recv()
+    west[lines] = east_in[...]
+    part = 3 * seg // 4
+    lax.fori_loop(0, part, functools.partial(free_step, outer), 0)
+
+    @pl.when(w == 1)
+    def _():
+        for l in inner:
+            take(l)
+
+    lax.fori_loop(part, seg, functools.partial(free_step, outer), 0)
+    begin(outer)
 
     def first_sums(i, acc):
         l, k = element(i)
@@ -269,17 +299,15 @@
     def _():
         cpack[...] = jnp.zeros_like(cpack)
 
+    @pl.when(w > 1)
+    def _():
+        for l in inner:
+            take(l)
+
     @pl.when(w > 0)
     def _():
-        for l in range(lines):
-            chain[l].wait_recv()
-            high, low = split(cin[l])
-            cpack[l] = jnp.concatenate([high, high, low], axis=0)
-
-            @pl.when(w < walls - 1)
-            def _():
-                cout[l] = carry_f[l] + left_t(mt[l], cpack[l])
-                chain[l].start()
+        for l in outer:
+            take(l)
 
     def correct(i, acc):
         l, k = element(i)

time: 44.3 us -> 42.7 us (0.964)
  Pallas kernels: 43.5 us -> 41.9 us
    pallas_call x1, Pallas kernels: 41.2 us -> 39.6 us  [per_device(): pl.pallas_call(functools.partial(kernel, sizes), out_shape=(pltpu.VMEM(ve...]
where the time goes in v3:
time: 42.7 us; the launch traced here: 42.5 us
  Pallas kernels  41.9 us (98%)
  between operations  0.64 us (1%)
    pallas_call x1, Pallas kernels, per_device(): pl.pallas_call(functools.partial(kernel, sizes), out_shape=(pltpu.VMEM(ve...  39.6 us
    pallas_call x1, Pallas kernels, per_device(): pl.pallas_call(finish, grid=(lines,), out_shape=(jax.ShapeDtypeStruct(vec...  2.3 us

profile of v3, /device:TPU:0, one launch (start us, length us, event | category | flops | bytes accessed | tf_op | source)
XLA Modules:
  0.0 42.5 jit_solution(1605073253571521699)
XLA Ops:
  0.6 39.6 %shard_map.77 = (bf16[4,4,320,256]{3,2,1,0:T(8,128)(2,1)S(1)}, f32[4,4,320,256]{3,2,1,0:T(8,128)S(1)}, f32[2,256]{1,0:T(2,128)S(1)}) custom-call(s32[4]{0:T(128)} %lengths.1, s32[1,4]{1,0:T(1,128)} %north_of.1, bf16[4,4,320,256]{3,2,1,0:T(8,128)(2,1)} %vector.1, bf16[4,4,320,320]{3,2,1,0:T(8,128)(2,1)} %diagonal.1, bf16[4,4,480,320]{3,2,1,0:T(8,128)(2,1)} %bitcast.1, ...), custom_call_target="tpu_custom_call" | custom-call | tf_op jit(solution)/shard_map/pallas_call | solution.py:384
  40.2 2.3 %shard_map.78 = (bf16[4,4,320,256]{3,2,1,0:T(8,128)(2,1)}, f32[2,256]{1,0:T(2,128)}) custom-call(bf16[4,4,320,256]{3,2,1,0:T(8,128)(2,1)S(1)} %get-tuple-element.5.masked, f32[4,4,320,256]{3,2,1,0:T(8,128)S(1)} %get-tuple-element.6.eliminated, f32[2,256]{1,0:T(2,128)S(1)} %get-tuple-element.7.stats), custom_call_target="tpu_custom_call" | custom-call | tf_op jit(solution)/shard_map/pallas_call | solution.py:434
